TPU v7x, 256 devices: a whole 4x4x8 slice. The times are simulated.
256 devices in a mesh: section: 8 (over x, core), seq: 32 (over z, y).
Axes of the slice: x: 4, y: 4, z: 8, core: 2. Of those that a mesh axis runs over, the one named last changes fastest.
Arguments:
- incoming: bfloat16 [4, 32, 16, 24, 320], P(None, 'seq'), may hold values from -6 to 6
- plan: int32 [4], replicated, may hold values from 0 to 3, each once
- waiting: bfloat16 [8, 32, 16, 24, 320], P('section', 'seq'), may hold values from -6 to 6
- spatial_weight: bfloat16 [8, 2, 9, 320, 320], P('section'), may hold values from -0.109375 to 0.109375
- temporal_weight: bfloat16 [8, 2, 3, 320, 320], P('section'), may hold values from -0.1875 to 0.1875
- attn_in: bfloat16 [8, 320, 960], P('section'), may hold values from -5 to 5
- attn_out: bfloat16 [8, 320, 320], P('section'), may hold values from -0.3125 to 0.3125
Outputs:
- outputs: bfloat16 [3, 8, 32, 16, 24, 320], P(None, 'section', 'seq')
Inputs may be any that keep to these rules, and one draw needn't show every extreme that they name: `plan`: each of the 4 clip numbers appears once.
All inputs are finite; a program needn't handle non-finite values.
Results may differ from a plain program's by a relative error of at most 0.02.
Values may be sent and summed in bfloat16 or wider, within the bound.
A program may use at most 64 MiB of HBM per device.

v0:
```python
import functools

import jax
import jax.numpy as jnp
from jax import lax
from jax.experimental import pallas as pl
from jax.experimental.pallas import tpu as pltpu
from jax.sharding import PartitionSpec as P

HEADS = 5
TICKS = 3
SEQ = 32
SECTIONS = 8
EPSILON = 1e-05
C = 320
CM = 256
CT = 64
W = 24
H = 16
CELLS = H * W
NA = 8
NB = 4
ROWS_A = SEQ * NA
ROWS_B = SEQ * NB
FAR = -1e30
MESH = pl.DeviceIdType.MESH
F32 = jnp.float32
BF16 = jnp.bfloat16


def dot(a, b):
    return jnp.dot(a, b, preferred_element_type=F32)


def silu(v):
    return v * (0.5 * jnp.tanh(0.5 * v) + 0.5)


def layer_norm(v):
    center = jnp.mean(v, axis=-1, keepdims=True)
    d = v - center
    spread = jnp.mean(d * d, axis=-1, keepdims=True)
    return d * lax.rsqrt(spread + EPSILON)


def group_norm(v, groups):
    count = 1.0 / (v.shape[0] * 10)

    def over_group(rows):
        wide = jnp.broadcast_to(rows, (8, C))
        total = jnp.dot(wide, groups, preferred_element_type=F32, precision=lax.Precision.HIGHEST)
        return total[0:1] * count

    center = over_group(jnp.sum(v, axis=0, keepdims=True))
    d = v - center
    spread = over_group(jnp.sum(d * d, axis=0, keepdims=True))
    return d * lax.rsqrt(spread + EPSILON)


def tails(a, b, c):
    zero = jnp.zeros_like(a)
    first = jnp.concatenate([a, zero], axis=1) + pltpu.roll(jnp.concatenate([b, zero], axis=1), CT, 1)
    return jnp.concatenate([first, c], axis=1)


def fill_taps(y, x_ref):
    main = y[:, :CM].astype(BF16)
    x_ref[W:, 0:CM] = main[: CELLS - W]
    x_ref[:, CM : 2 * CM] = main
    x_ref[: CELLS - W, 2 * CM : 3 * CM] = main[W:]
    tail = y[:, CM:]
    edge = jnp.zeros((W, CT), F32)
    above = jnp.concatenate([edge, tail[: CELLS - W]], axis=0)
    below = jnp.concatenate([tail[W:], edge], axis=0)
    x_ref[:, 3 * CM :] = tails(above, tail, below).astype(BF16)


def column_taps(p):
    rows = p.shape[0]
    high = rows // W

    def add(left, mid, right):
        width = left.shape[1]
        col = lax.broadcasted_iota(jnp.int32, (high, W, width), 1)
        left = pltpu.roll(left, 1, 0).reshape(high, W, width)
        right = pltpu.roll(right, rows - 1, 0).reshape(high, W, width)
        left = jnp.where(col > 0, left, 0.0).reshape(rows, width)
        right = jnp.where(col < W - 1, right, 0.0).reshape(rows, width)
        return mid + left + right

    main = add(p[:, 0:CM], p[:, CM : 2 * CM], p[:, 2 * CM : 3 * CM])
    pair = p[:, 3 * CM : 3 * CM + 2 * CT]
    mid = pltpu.roll(pair, CT, 1)[:, :CT]
    tail = add(pair[:, :CT], mid, p[:, 3 * CM + 2 * CT :])
    return jnp.concatenate([main, tail], axis=1)


def temporal_dot(act, cells, w):
    rows = act.shape[0]
    row = lax.broadcasted_iota(jnp.int32, (rows, C), 0)
    before = jnp.where(row >= cells, pltpu.roll(act, cells, 0), 0.0)
    after = jnp.where(row < rows - cells, pltpu.roll(act, rows - cells, 0), 0.0)
    lhs = jnp.concatenate(
        [
            before[:, :CM].astype(BF16),
            act[:, :CM].astype(BF16),
            after[:, :CM].astype(BF16),
            tails(before[:, CM:], act[:, CM:], after[:, CM:]).astype(BF16),
        ],
        axis=1,
    )
    return dot(lhs, w)


def temporal_part(x1, cells, tw_ref, wi_ref, wo_ref, bias_ref):
    rows = x1.shape[0]
    x1 = x1.astype(F32)
    u = temporal_dot(silu(layer_norm(x1)), cells, tw_ref[0]).astype(BF16).astype(F32)
    x2 = (x1 + temporal_dot(silu(layer_norm(u)), cells, tw_ref[1])).astype(BF16).astype(F32)
    proj = dot(layer_norm(x2).astype(BF16), wi_ref[...])
    lane = lax.broadcasted_iota(jnp.int32, (rows, 2 * CT), 1)
    low = lane < CT
    bias = bias_ref[...]
    scale = 0.125 * 1.4426950408889634

    def weights(q, k):
        s = lax.dot_general(q, k, (((1,), (1,)), ((), ())), preferred_element_type=F32) + bias
        top = jnp.max(s, axis=-1, keepdims=True)
        return jnp.exp2((s - top) * scale).astype(BF16)

    mixed = []
    for pair in range(3):
        q = proj[:, 128 * pair : 128 * pair + 128]
        k = proj[:, 384 + 128 * pair : 512 + 128 * pair].astype(BF16)
        if pair < 2:
            v = proj[:, 768 + 128 * pair : 896 + 128 * pair]
        else:
            v = pltpu.roll(q, CT, 1)
        even = dot(weights(jnp.where(low, q, 0.0).astype(BF16), k), jnp.where(low, v, 1.0).astype(BF16))
        if pair < 2:
            odd = dot(weights(jnp.where(low, 0.0, q).astype(BF16), k), jnp.where(low, 1.0, v).astype(BF16))
            total = pltpu.roll(jnp.where(low, odd, even), CT, 1)
            mixed.append((jnp.where(low, even, odd) / total).astype(BF16))
        else:
            mixed.append((even / pltpu.roll(even, CT, 1)).astype(BF16)[:, :CT])
    mixed = jnp.concatenate(mixed, axis=1)
    return (x2 + dot(mixed, wo_ref[...])).astype(BF16)


def body(
    inc_hbm, plan, wait_hbm, sw_hbm, tw_hbm, ai_hbm, ao_hbm, out_hbm,
    inc, xi, xs, sw, tw, ai, ao, wc, wi, groups, bias_a, bias_b, taps,
    sa, sb, fa, fb, ta, tb, ra, rb,
    in_sem, fs_sem, fr_sem, rs_sem, rr_sem, os_sem, or_sem,
):
    me = lax.axis_index("seq")
    section = lax.axis_index("section")
    nxt = lax.rem(section + 1, SECTIONS)
    prv = lax.rem(section + SECTIONS - 1, SECTIONS)

    loads = [
        pltpu.make_async_copy(wait_hbm, xi, in_sem.at[0]),
        pltpu.make_async_copy(sw_hbm.at[0], sw.at[0], in_sem.at[1]),
        pltpu.make_async_copy(sw_hbm.at[1], sw.at[1], in_sem.at[2]),
        pltpu.make_async_copy(ai_hbm, ai, in_sem.at[3]),
        pltpu.make_async_copy(ao_hbm, ao, in_sem.at[4]),
        pltpu.make_async_copy(inc_hbm, inc, in_sem.at[5]),
    ]
    slot = 6
    for k in range(2):
        for i in range(3):
            loads.append(pltpu.make_async_copy(
                tw_hbm.at[k, i, pl.ds(0, CM)], tw.at[k, pl.ds(CM * i, CM)], in_sem.at[slot]))
            loads.append(pltpu.make_async_copy(
                tw_hbm.at[k, i, pl.ds(CM, CT)], tw.at[k, pl.ds(3 * CM + CT * i, CT)], in_sem.at[slot + 1]))
            slot += 2
    for load in loads:
        load.start()

    barrier = pltpu.get_barrier_semaphore()

    def greet(k, carry):
        pl.semaphore_signal(barrier, 1, device_id={"section": nxt, "seq": k}, device_id_type=MESH)

        @pl.when(k != me)
        def _():
            pl.semaphore_signal(barrier, 1, device_id={"section": section, "seq": k}, device_id_type=MESH)

        return carry

    lax.fori_loop(0, SEQ, greet, 0)
    pl.semaphore_signal(barrier, 1, device_id={"section": prv, "seq": me}, device_id_type=MESH)

    row = lax.broadcasted_iota(jnp.int32, (C, C), 0)
    col = lax.broadcasted_iota(jnp.int32, (C, C), 1)
    groups[...] = jnp.where((row * 6554) // 65536 == (col * 6554) // 65536, 1.0, 0.0)
    taps[...] = jnp.zeros_like(taps)
    for ref, cells in ((bias_a, NA), (bias_b, NB)):
        r = lax.broadcasted_iota(jnp.int32, ref.shape, 0)
        c = lax.broadcasted_iota(jnp.int32, ref.shape, 1)
        ref[...] = jnp.where((r & (cells - 1)) == (c & (cells - 1)), 0.0, FAR)

    def pack_conv(k):
        for i in range(3):
            part = [sw[k, 3 * i + j] for j in range(3)]
            side = tails(*[t[:, CM:].astype(F32) for t in part]).astype(BF16)
            whole = jnp.concatenate([t[:, :CM] for t in part] + [side], axis=1)
            wc[k, CM * i : CM * i + CM] = whole[:CM]
            wc[k, 3 * CM + CT * i : 3 * CM + CT * i + CT] = whole[CM:]

    def pack_attn():
        whole = ai[...].astype(F32)
        q = whole[:, :256]
        cross = whole[:, 256:384]
        mid = whole[:, 384:640]
        v = whole[:, 640:896]
        last = jnp.concatenate([whole[:, 896:960], jnp.zeros((C, CT), F32)], axis=1)
        low = lax.broadcasted_iota(jnp.int32, (C, 128), 1) < CT
        turned = [pltpu.roll(t, CT, 1) for t in (cross, mid[:, :128], mid[:, 128:])]
        wi[:, 0:256] = q.astype(BF16)
        wi[:, 256:384] = jnp.where(low, cross, pltpu.roll(last, CT, 1)).astype(BF16)
        wi[:, 384:512] = jnp.where(low, turned[0], turned[1]).astype(BF16)
        wi[:, 512:640] = jnp.where(low, turned[1], turned[2]).astype(BF16)
        wi[:, 640:768] = jnp.where(low, turned[2], 0.0).astype(BF16)
        wi[:, 768:1024] = v.astype(BF16)

    def send_forward(t, src, dst, lane):
        def one(k, carry):
            to = lax.rem(me + k, SEQ)
            pltpu.make_async_remote_copy(
                src.at[t, to], dst.at[t, me], fs_sem.at[lane, t], fr_sem.at[lane, t],
                device_id={"section": section, "seq": to}, device_id_type=MESH).start()
            return carry

        pltpu.make_async_copy(src.at[t, me], dst.at[t, me], fr_sem.at[lane, t]).start()
        lax.fori_loop(1, SEQ, one, 0)

    def send_back(t, src, dst, lane):
        target = jnp.where(t < TICKS - 1, nxt, section)

        def one(k, carry):
            to = lax.rem(me + k, SEQ)
            pltpu.make_async_remote_copy(
                src.at[t, to], dst.at[t, me], rs_sem.at[lane, t], rr_sem.at[lane, t],
                device_id={"section": target, "seq": to}, device_id_type=MESH).start()
            return carry

        @pl.when(t < TICKS - 1)
        def _():
            one(0, 0)

        @pl.when(t == TICKS - 1)
        def _():
            pltpu.make_async_copy(src.at[t, me], dst.at[t, me], rr_sem.at[lane, t]).start()

        lax.fori_loop(1, SEQ, one, 0)

    def whole(ref, sem):
        pltpu.make_async_copy(ref, ref, sem).wait()

    loads[0].wait()

    def tick(t, carry):
        x = xi[...].astype(F32)
        fill_taps(silu(group_norm(x, groups[...])), taps)

        @pl.when(t == 0)
        def _():
            loads[1].wait()
            pack_conv(0)
            loads[2].wait()
            pack_conv(1)

        a = column_taps(dot(taps[...], wc[0])).astype(BF16).astype(F32)
        fill_taps(silu(group_norm(a, groups[...])), taps)
        got = column_taps(dot(taps[0 : 11 * W], wc[1]))
        sa[t] = (x[:ROWS_A] + got[:ROWS_A]).astype(BF16).reshape(SEQ, NA, C)

        @pl.when(t == 0)
        def _():
            pl.semaphore_wait(barrier, 2 * SEQ)

        send_forward(t, sa, fa, 0)
        got = column_taps(dot(taps[10 * W :], wc[1]))
        sb[t] = (x[ROWS_A:] + got[ROWS_A - 10 * W :]).astype(BF16).reshape(SEQ, NB, C)
        send_forward(t, sb, fb, 1)

        @pl.when(t == 0)
        def _():
            for load in loads[3:]:
                load.wait()
            pack_attn()

        whole(fa.at[t], fr_sem.at[0, t])
        done = temporal_part(fa[t].reshape(ROWS_A, C), NA, tw, wi, ao, bias_a)
        ta[t] = done.reshape(SEQ, NA, C)
        send_back(t, ta, ra, 0)
        whole(fb.at[t], fr_sem.at[1, t])
        done = temporal_part(fb[t].reshape(ROWS_B, C), NB, tw, wi, ao, bias_b)
        tb[t] = done.reshape(SEQ, NB, C)
        send_back(t, tb, rb, 1)
        whole(ra.at[t], rr_sem.at[0, t])
        whole(rb.at[t], rr_sem.at[1, t])
        xs[t, 0:ROWS_A] = ra[t].reshape(ROWS_A, C)
        xs[t, ROWS_A:] = rb[t].reshape(ROWS_B, C)

        @pl.when(t < TICKS - 1)
        def _():
            pltpu.make_async_remote_copy(
                xs.at[t], out_hbm.at[t], os_sem.at[t], or_sem.at[t],
                device_id={"section": prv, "seq": me}, device_id_type=MESH).start()
            xi[...] = jnp.where(section == 0, inc[plan[t]], xs[t])

        return carry

    lax.fori_loop(0, TICKS, tick, 0)
    last = pltpu.make_async_copy(xs.at[TICKS - 1], out_hbm.at[TICKS - 1], os_sem.at[TICKS - 1])
    last.start()
    for t in range(TICKS):
        for lane, (src, back) in enumerate(((sa, ta), (sb, tb))):
            part = src.at[t, pl.ds(0, SEQ - 1)]
            pltpu.make_async_copy(part, part, fs_sem.at[lane, t]).wait()
            part = back.at[t, pl.ds(0, SEQ - 1 if t == TICKS - 1 else SEQ)]
            pltpu.make_async_copy(part, part, rs_sem.at[lane, t]).wait()
    for t in range(TICKS - 1):
        pltpu.make_async_copy(xs.at[t], xs.at[t], os_sem.at[t]).wait()
        pltpu.make_async_copy(out_hbm.at[t], out_hbm.at[t], or_sem.at[t]).wait()
    last.wait()


def shards(incoming, plan, waiting, spatial_weight, temporal_weight, attn_in, attn_out):
    hbm = pl.BlockSpec(memory_space=pl.ANY)
    steps = (TICKS,)
    out = pl.pallas_call(
        body,
        out_shape=jax.ShapeDtypeStruct((TICKS, CELLS, C), BF16),
        in_specs=[hbm, pl.BlockSpec(memory_space=pltpu.SMEM), hbm, hbm, hbm, hbm, hbm],
        out_specs=hbm,
        scratch_shapes=[
            pltpu.VMEM((4, CELLS, C), BF16),
            pltpu.VMEM((CELLS, C), BF16),
            pltpu.VMEM(steps + (CELLS, C), BF16),
            pltpu.VMEM((2, 9, C, C), BF16),
            pltpu.VMEM((2, 3 * C, C), BF16),
            pltpu.VMEM((C, 3 * C), BF16),
            pltpu.VMEM((C, C), BF16),
            pltpu.VMEM((2, 3 * C, 3 * C), BF16),
            pltpu.VMEM((C, 1024), BF16),
            pltpu.VMEM((C, C), F32),
            pltpu.VMEM((ROWS_A, ROWS_A), F32),
            pltpu.VMEM((ROWS_B, ROWS_B), F32),
            pltpu.VMEM((CELLS, 3 * C), BF16),
        ]
        + [pltpu.VMEM(steps + (SEQ, n, C), BF16) for _ in range(4) for n in (NA, NB)]
        + [
            pltpu.SemaphoreType.DMA((18,)),
            pltpu.SemaphoreType.DMA((2, TICKS)),
            pltpu.SemaphoreType.DMA((2, TICKS)),
            pltpu.SemaphoreType.DMA((2, TICKS)),
            pltpu.SemaphoreType.DMA((2, TICKS)),
            pltpu.SemaphoreType.DMA((TICKS,)),
            pltpu.SemaphoreType.DMA((TICKS,)),
        ],
        compiler_params=pltpu.CompilerParams(
            collective_id=0, has_side_effects=True, vmem_limit_bytes=60 * 1024 * 1024),
    )(
        incoming.reshape(4, CELLS, C), plan, waiting.reshape(CELLS, C),
        spatial_weight[0], temporal_weight[0], attn_in[0], attn_out[0],
    )
    return out.reshape(TICKS, 1, 1, H, W, C)


def solution(mesh):
    return jax.shard_map(
        shards,
        mesh=mesh,
        in_specs=(
            P(None, "seq", None, None, None),
            P(),
            P("section", "seq", None, None, None),
            P("section", None, None, None, None),
            P("section", None, None, None, None),
            P("section", None, None),
            P("section", None, None),
        ),
        out_specs=P(None, "section", "seq", None, None, None),
        check_vma=False,
    )
```

profile of v0, /device:TPU:32, one launch (start us, length us, event | category | flops | bytes accessed | tf_op | source)
XLA Modules:
  0.0 87.8 jit_solution(16760607858246317300)
XLA Ops:
  0.0 85.6 %shard_map.73 = bf16[3,384,320]{2,1,0:T(8,128)(2,1)} custom-call(bf16[4,384,320]{2,1,0:T(8,128)(2,1)} %bitcast.12, s32[4]{0:T(128)} %plan.1, bf16[384,320]{1,0:T(8,128)(2,1)} %bitcast.14, bf16[2,9,320,320]{3,2,1,0:T(8,128)(2,1)} %bitcast.9, bf16[2,3,320,320]{3,2,1,0:T(8,128)(2,1)} %bitcast.11, bf16[320,960]{1,0:T(8,128)(2,1)} %bitcast.13, ...), custom_call_target="tpu_custom_call" | custom-call | tf_op jit(solution)/shard_map/pallas_call | solution.py:334
  85.7 2.2 %copy.10 = bf16[3,1,1,16,24,320]{5,4,3,2,1,0:T(8,128)(2,1)} copy(bf16[3,1,1,16,24,320]{5,4,3,2,1,0:T(8,128)(2,1)} %bitcast.10) | data formatting | bytes 1474560
where the time goes:
time: 87.9 us; the launch traced here: 87.8 us
  Pallas kernels  85.6 us (97%)
  local copies, waits for them, and re-layouts  2.17 us (2%)
    pallas_call x1, Pallas kernels, shards(): pl.pallas_call(body, out_shape=jax.ShapeDtypeStruct((TICKS, CELLS, C), BF...  85.6 us
    unnamed x1, local copies, waits for them, and re-layouts  2.17 us

commit v1 on v0

v1 whole, which is shorter than its diff:
```python
import jax
import jax.numpy as jnp
from jax import lax
from jax.experimental import pallas as pl
from jax.experimental.pallas import tpu as pltpu
from jax.sharding import PartitionSpec as P

TICKS = 3
SEQ = 32
NY = 4
NZ = 8
SECTIONS = 8
EPSILON = 1e-05
C = 320
CM = 256
CT = 64
W = 24
H = 16
CELLS = H * W
NA = 4
NB = 2
ROWS_A = SEQ * NA * 2
ROWS_B = SEQ * NB * 2
BLOCK = 128
PIVOT = ROWS_A
FAR = -1e30
MESH = pl.DeviceIdType.MESH
F32 = jnp.float32
BF16 = jnp.bfloat16


def hops(offset):
    dz, dy = offset
    return min(dz, NZ - dz) + min(dy, NY - dy)


OFFSETS = sorted(
    [(dz, dy) for dz in range(NZ) for dy in range(NY) if (dz, dy) != (0, 0)], key=lambda o: -hops(o)
)


def dot(a, b):
    return jnp.dot(a, b, preferred_element_type=F32)


def silu_of_half(h):
    return h * jnp.tanh(h) + h


def layer_norm(v, factor):
    center = jnp.mean(v, axis=-1, keepdims=True)
    d = v - center
    spread = jnp.mean(d * d, axis=-1, keepdims=True)
    return d * (factor * lax.rsqrt(spread + EPSILON))


def over_groups(rows, groups):
    high = rows.astype(BF16).astype(F32)
    rest = rows - high
    mid = rest.astype(BF16).astype(F32)
    low = rest - mid
    parts = jnp.concatenate([high, mid, low, jnp.zeros_like(low)], axis=0).astype(BF16)
    got = dot(parts, groups)
    return got[0:2] + got[2:4] + got[4:6]


def find_pivot(v, groups):
    total = jnp.sum(v, axis=0, keepdims=True)
    return over_groups(jnp.concatenate([total, total], axis=0), groups)[0:1] * (1.0 / (v.shape[0] * 10))


def group_norm_half(v, pivot, groups):
    count = 1.0 / (CELLS * 10)
    d = v - pivot
    sums = jnp.concatenate([jnp.sum(d, axis=0, keepdims=True), jnp.sum(d * d, axis=0, keepdims=True)], axis=0)
    means = over_groups(sums, groups) * count
    shift = means[0:1]
    spread = jnp.maximum(means[1:2] - shift * shift, 0.0)
    scale = 0.5 * lax.rsqrt(spread + EPSILON)
    return d * scale - shift * scale


def side_by_side(a, b):
    zero = jnp.zeros_like(a)
    return jnp.concatenate([a, zero], axis=1) + pltpu.roll(jnp.concatenate([b, zero], axis=1), CT, 1)


def tails(a, b, c):
    return jnp.concatenate([side_by_side(a, b), c], axis=1)


def fill_taps(y, x_ref):
    main = y[:, :CM].astype(BF16)
    x_ref[W:, 0:CM] = main[: CELLS - W]
    x_ref[:, CM : 2 * CM] = main
    x_ref[: CELLS - W, 2 * CM : 3 * CM] = main[W:]
    tail = y[:, CM:]
    edge = jnp.zeros((W, CT), F32)
    above = jnp.concatenate([edge, tail[: CELLS - W]], axis=0)
    below = jnp.concatenate([tail[W:], edge], axis=0)
    x_ref[:, 3 * CM :] = tails(above, tail, below).astype(BF16)


def column_taps(p):
    rows = p.shape[0]
    high = rows // W

    def add(left, mid, right):
        width = left.shape[1]
        col = lax.broadcasted_iota(jnp.int32, (high, W, width), 1)
        left = pltpu.roll(left, 1, 0).reshape(high, W, width)
        right = pltpu.roll(right, rows - 1, 0).reshape(high, W, width)
        left = jnp.where(col > 0, left, 0.0).reshape(rows, width)
        right = jnp.where(col < W - 1, right, 0.0).reshape(rows, width)
        return mid + left + right

    main = add(p[:, 0:CM], p[:, CM : 2 * CM], p[:, 2 * CM : 3 * CM])
    pair = p[:, 3 * CM : 3 * CM + 2 * CT]
    mid = pltpu.roll(pair, CT, 1)[:, :CT]
    tail = add(pair[:, :CT], mid, p[:, 3 * CM + 2 * CT :])
    return jnp.concatenate([main, tail], axis=1)


def pack(v):
    half = v.shape[0] // 2
    low, high = v[:half], v[half:]
    return jnp.concatenate(
        [low[:, :CM].astype(BF16), high[:, :CM].astype(BF16), side_by_side(low[:, CM:], high[:, CM:]).astype(BF16)],
        axis=1,
    )


def unpack(p):
    p = p.astype(F32)
    side = p[:, 2 * CM :]
    low = jnp.concatenate([p[:, :CM], side[:, :CT]], axis=1)
    high = jnp.concatenate([p[:, CM : 2 * CM], pltpu.roll(side, CT, 1)[:, :CT]], axis=1)
    return jnp.concatenate([low, high], axis=0)


def temporal_dot(act, cells, w):
    rows = act.shape[0]
    half = rows // 2
    row = lax.broadcasted_iota(jnp.int32, (rows, C), 0) & (half - 1)
    before = jnp.where(row >= cells, pltpu.roll(act, cells, 0), 0.0)
    after = jnp.where(row < half - cells, pltpu.roll(act, rows - cells, 0), 0.0)
    lhs = jnp.concatenate(
        [
            before[:, :CM].astype(BF16),
            act[:, :CM].astype(BF16),
            after[:, :CM].astype(BF16),
            tails(before[:, CM:], act[:, CM:], after[:, CM:]).astype(BF16),
        ],
        axis=1,
    )
    return dot(lhs, w)


def attention(proj, bias):
    low = lax.broadcasted_iota(jnp.int32, (BLOCK, 2 * CT), 1) < CT
    scale = 0.125 * 1.4426950408889634
    scores, held = [], []
    for pair in range(3):
        q = proj[:, 128 * pair : 128 * pair + 128]
        k = proj[:, 384 + 128 * pair : 512 + 128 * pair].astype(BF16)
        v = proj[:, 768 + 128 * pair : 896 + 128 * pair] if pair < 2 else pltpu.roll(q, CT, 1)
        for side in range(2 if pair < 2 else 1):
            own = low if side == 0 else jnp.logical_not(low)
            one = jnp.where(own, q, 0.0).astype(BF16)
            scores.append(lax.dot_general(one, k, (((1,), (1,)), ((), ())), preferred_element_type=F32) + bias)
            held.append(jnp.where(own, v, 1.0).astype(BF16))
    tops = [jnp.max(s, axis=-1, keepdims=True) for s in scores]
    weights = [jnp.exp2((s - top) * scale).astype(BF16) for s, top in zip(scores, tops)]
    got = [dot(w, v) for w, v in zip(weights, held)]
    mixed = []
    for pair in range(2):
        even, odd = got[2 * pair], got[2 * pair + 1]
        total = pltpu.roll(jnp.where(low, odd, even), CT, 1)
        mixed.append((jnp.where(low, even, odd) / total).astype(BF16))
    mixed.append((got[4] / pltpu.roll(got[4], CT, 1)).astype(BF16)[:, :CT])
    return jnp.concatenate(mixed, axis=1)


def temporal_part(x1, cells, tw_ref, wi_ref, wo_ref, bias_ref):
    u = temporal_dot(silu_of_half(layer_norm(x1, 0.5)), cells, tw_ref[0]).astype(BF16).astype(F32)
    x2 = (x1 + temporal_dot(silu_of_half(layer_norm(u, 0.5)), cells, tw_ref[1])).astype(BF16).astype(F32)
    proj = dot(layer_norm(x2, 1.0).astype(BF16), wi_ref[...])
    bias = bias_ref[...]
    mixed = [attention(proj[at : at + BLOCK], bias) for at in range(0, x1.shape[0], BLOCK)]
    mixed = mixed[0] if len(mixed) == 1 else jnp.concatenate(mixed, axis=0)
    return x2 + dot(mixed, wo_ref[...])


def body(
    inc_hbm, plan, wait_hbm, sw_hbm, tw_hbm, ai_hbm, ao_hbm, out0, out1, out2,
    inc, xi, xs, sw, tw, ai, ao, wc, wi, groups, pivot, bias_a, bias_b, taps,
    sa, sb, fa, fb, ta, tb, ra, rb,
    in_sem, fs_sem, fr_sem, rs_sem, rr_sem, os_sem, or_sem, ready,
):
    me = lax.axis_index("seq")
    section = lax.axis_index("section")
    nxt = lax.rem(section + 1, SECTIONS)
    prv = lax.rem(section + SECTIONS - 1, SECTIONS)
    my_z = me // NY
    my_y = lax.rem(me, NY)

    def peer(offset):
        dz, dy = offset
        return lax.rem(my_z + dz, NZ) * NY + lax.rem(my_y + dy, NY)

    barrier = pltpu.get_barrier_semaphore()
    for offset in OFFSETS:
        pl.semaphore_signal(barrier, 1, device_id={"section": section, "seq": peer(offset)}, device_id_type=MESH)
    for other in (nxt, prv):
        pl.semaphore_signal(barrier, 1, device_id={"section": other, "seq": me}, device_id_type=MESH)

    loads = [
        pltpu.make_async_copy(wait_hbm, xi, in_sem.at[0]),
        pltpu.make_async_copy(sw_hbm.at[0], sw.at[0], in_sem.at[1]),
        pltpu.make_async_copy(sw_hbm.at[1], sw.at[1], in_sem.at[2]),
        pltpu.make_async_copy(ai_hbm, ai, in_sem.at[3]),
        pltpu.make_async_copy(ao_hbm, ao, in_sem.at[4]),
        pltpu.make_async_copy(inc_hbm, inc, in_sem.at[5]),
    ]
    slot = 6
    for k in range(2):
        for i in range(3):
            loads.append(pltpu.make_async_copy(
                tw_hbm.at[k, i, pl.ds(0, CM)], tw.at[k, pl.ds(CM * i, CM)], in_sem.at[slot]))
            loads.append(pltpu.make_async_copy(
                tw_hbm.at[k, i, pl.ds(CM, CT)], tw.at[k, pl.ds(3 * CM + CT * i, CT)], in_sem.at[slot + 1]))
            slot += 2
    for load in loads:
        load.start()

    row = lax.broadcasted_iota(jnp.int32, (C, C), 0)
    col = lax.broadcasted_iota(jnp.int32, (C, C), 1)
    groups[...] = jnp.where((row * 6554) // 65536 == (col * 6554) // 65536, 1.0, 0.0).astype(BF16)
    taps[0:W, 0:CM] = jnp.zeros((W, CM), BF16)
    taps[CELLS - W :, 2 * CM : 3 * CM] = jnp.zeros((W, CM), BF16)

    def make_bias():
        r = lax.broadcasted_iota(jnp.int32, (BLOCK, BLOCK), 0)
        c = lax.broadcasted_iota(jnp.int32, (BLOCK, BLOCK), 1)
        bias_a[...] = jnp.where((r & (NA - 1)) == (c & (NA - 1)), 0.0, FAR)
        half = SEQ * NB
        same = ((r & (NB - 1)) == (c & (NB - 1))) & ((r & half) == (c & half))
        bias_b[...] = jnp.where(same, 0.0, FAR)

    def pack_conv(k):
        for i in range(3):
            part = [sw[k, 3 * i + j] for j in range(3)]
            side = tails(*[t[:, CM:].astype(F32) for t in part]).astype(BF16)
            whole = jnp.concatenate([t[:, :CM] for t in part] + [side], axis=1)
            wc[k, CM * i : CM * i + CM] = whole[:CM]
            wc[k, 3 * CM + CT * i : 3 * CM + CT * i + CT] = whole[CM:]

    def pack_attn():
        whole = ai[...].astype(F32)
        cross = whole[:, 256:384]
        mid = whole[:, 384:640]
        last = jnp.concatenate([whole[:, 896:960], jnp.zeros((C, CT), F32)], axis=1)
        low = lax.broadcasted_iota(jnp.int32, (C, 128), 1) < CT
        turned = [pltpu.roll(t, CT, 1) for t in (cross, mid[:, :128], mid[:, 128:])]
        wi[:, 0:256] = ai[:, :256]
        wi[:, 256:384] = jnp.where(low, cross, pltpu.roll(last, CT, 1)).astype(BF16)
        wi[:, 384:512] = jnp.where(low, turned[0], turned[1]).astype(BF16)
        wi[:, 512:640] = jnp.where(low, turned[1], turned[2]).astype(BF16)
        wi[:, 640:768] = jnp.where(low, turned[2], 0.0).astype(BF16)
        wi[:, 768:1024] = ai[:, 640:896]

    def send_all(t, src, dst, to_section, send_sem, recv_sem):
        for offset in OFFSETS:
            to = peer(offset)
            pltpu.make_async_remote_copy(
                src.at[t, to], dst.at[t, me], send_sem, recv_sem,
                device_id={"section": to_section, "seq": to}, device_id_type=MESH).start()

    def send_forward(t, src, dst, lane):
        send_all(t, src, dst, section, fs_sem.at[lane, t], fr_sem.at[lane, t])
        pltpu.make_async_copy(src.at[t, me], dst.at[t, me], fr_sem.at[lane, t]).start()

    def send_back(t, src, dst, lane):
        target = jnp.where(t < TICKS - 1, nxt, section)
        send_all(t, src, dst, target, rs_sem.at[lane, t], rr_sem.at[lane, t])

        @pl.when(t < TICKS - 1)
        def _():
            pltpu.make_async_remote_copy(
                src.at[t, me], dst.at[t, me], rs_sem.at[lane, t], rr_sem.at[lane, t],
                device_id={"section": target, "seq": me}, device_id_type=MESH).start()

        @pl.when(t == TICKS - 1)
        def _():
            pltpu.make_async_copy(src.at[t, me], dst.at[t, me], rr_sem.at[lane, t]).start()

    def whole(ref, sem):
        pltpu.make_async_copy(ref, ref, sem).wait()

    loads[0].wait()
    pivot[...] = find_pivot(xi[:PIVOT].astype(F32), groups[...])

    def tick(t, carry):
        x = xi[...].astype(F32)
        fill_taps(silu_of_half(group_norm_half(x, pivot[...], groups[...])), taps)

        @pl.when(t == 0)
        def _():
            loads[1].wait()
            pack_conv(0)
            loads[2].wait()
            pack_conv(1)

        top = 11 * W
        a = column_taps(dot(taps[...], wc[0])).astype(BF16).astype(F32)
        fill_taps(silu_of_half(group_norm_half(a, find_pivot(a[:PIVOT], groups[...]), groups[...])), taps)
        got = column_taps(dot(taps[0:top], wc[1]))
        sa[t] = pack(x[:ROWS_A] + got[:ROWS_A]).reshape(SEQ, NA, 2 * C)

        @pl.when(t == 0)
        def _():
            pl.semaphore_wait(barrier, SEQ + 1)

        send_forward(t, sa, fa, 0)
        got = column_taps(dot(taps[top - W :], wc[1]))
        sb[t] = pack(x[ROWS_A:] + got[ROWS_A - top + W :]).reshape(SEQ, NB, 2 * C)
        send_forward(t, sb, fb, 1)

        @pl.when(t == 0)
        def _():
            make_bias()
            for load in loads[3:]:
                load.wait()
            pack_attn()

        whole(fa.at[t], fr_sem.at[0, t])

        @pl.when(t == 0)
        def _():
            pl.semaphore_signal(ready, 1, device_id={"section": prv, "seq": me}, device_id_type=MESH)

        done = temporal_part(unpack(fa[t].reshape(SEQ * NA, 2 * C)), NA, tw, wi, ao, bias_a)
        ta[t] = pack(done).reshape(SEQ, NA, 2 * C)

        @pl.when(t == 0)
        def _():
            pl.semaphore_wait(ready, 1)

        send_back(t, ta, ra, 0)
        whole(fb.at[t], fr_sem.at[1, t])
        done = temporal_part(unpack(fb[t].reshape(SEQ * NB, 2 * C)), NB, tw, wi, ao, bias_b)
        tb[t] = pack(done).reshape(SEQ, NB, 2 * C)
        send_back(t, tb, rb, 1)
        whole(ra.at[t], rr_sem.at[0, t])
        came = unpack(ra[t].reshape(SEQ * NA, 2 * C)).astype(BF16)
        xs[t, 0:ROWS_A] = came
        came = jnp.where(section == 0, inc[plan[t], 0:ROWS_A], came)
        xi[0:ROWS_A] = came
        pivot[...] = find_pivot(came.astype(F32), groups[...])
        whole(rb.at[t], rr_sem.at[1, t])
        came = unpack(rb[t].reshape(SEQ * NB, 2 * C)).astype(BF16)
        xs[t, ROWS_A:] = came

        for early, out_ref in enumerate((out0, out1)):
            @pl.when(t == early)
            def _(early=early, out_ref=out_ref):
                pltpu.make_async_remote_copy(
                    xs.at[early], out_ref, os_sem.at[early], or_sem.at[early],
                    device_id={"section": prv, "seq": me}, device_id_type=MESH).start()

        @pl.when(t < TICKS - 1)
        def _():
            xi[ROWS_A:] = jnp.where(section == 0, inc[plan[t], ROWS_A:], xs[t, ROWS_A:])

        return carry

    lax.fori_loop(0, TICKS, tick, 0)
    last = pltpu.make_async_copy(xs.at[TICKS - 1], out2, os_sem.at[TICKS - 1])
    last.start()
    for t in range(TICKS):
        for lane, (src, back) in enumerate(((sa, ta), (sb, tb))):
            part = src.at[t, pl.ds(0, SEQ - 1)]
            pltpu.make_async_copy(part, part, fs_sem.at[lane, t]).wait()
            part = back.at[t, pl.ds(0, SEQ - 1 if t == TICKS - 1 else SEQ)]
            pltpu.make_async_copy(part, part, rs_sem.at[lane, t]).wait()
    for t, out_ref in enumerate((out0, out1)):
        pltpu.make_async_copy(xs.at[t], xs.at[t], os_sem.at[t]).wait()
        pltpu.make_async_copy(out_ref, out_ref, or_sem.at[t]).wait()
    last.wait()


def shards(incoming, plan, waiting, spatial_weight, temporal_weight, attn_in, attn_out):
    hbm = pl.BlockSpec(memory_space=pl.ANY)
    steps = (TICKS,)
    out = pl.pallas_call(
        body,
        out_shape=[jax.ShapeDtypeStruct((CELLS, C), BF16)] * TICKS,
        in_specs=[hbm, pl.BlockSpec(memory_space=pltpu.SMEM), hbm, hbm, hbm, hbm, hbm],
        out_specs=[hbm] * TICKS,
        scratch_shapes=[
            pltpu.VMEM((4, CELLS, C), BF16),
            pltpu.VMEM((CELLS, C), BF16),
            pltpu.VMEM(steps + (CELLS, C), BF16),
            pltpu.VMEM((2, 9, C, C), BF16),
            pltpu.VMEM((2, 3 * C, C), BF16),
            pltpu.VMEM((C, 3 * C), BF16),
            pltpu.VMEM((C, C), BF16),
            pltpu.VMEM((2, 3 * C, 3 * C), BF16),
            pltpu.VMEM((C, 1024), BF16),
            pltpu.VMEM((C, C), BF16),
            pltpu.VMEM((1, C), F32),
            pltpu.VMEM((BLOCK, BLOCK), F32),
            pltpu.VMEM((BLOCK, BLOCK), F32),
            pltpu.VMEM((CELLS, 3 * C), BF16),
        ]
        + [pltpu.VMEM(steps + (SEQ, n, 2 * C), BF16) for _ in range(4) for n in (NA, NB)]
        + [
            pltpu.SemaphoreType.DMA((18,)),
            pltpu.SemaphoreType.DMA((2, TICKS)),
            pltpu.SemaphoreType.DMA((2, TICKS)),
            pltpu.SemaphoreType.DMA((2, TICKS)),
            pltpu.SemaphoreType.DMA((2, TICKS)),
            pltpu.SemaphoreType.DMA((TICKS,)),
            pltpu.SemaphoreType.DMA((TICKS,)),
            pltpu.SemaphoreType.REGULAR,
        ],
        compiler_params=pltpu.CompilerParams(
            collective_id=0, has_side_effects=True, vmem_limit_bytes=60 * 1024 * 1024),
    )(
        incoming.reshape(4, CELLS, C), plan, waiting.reshape(CELLS, C),
        spatial_weight[0], temporal_weight[0], attn_in[0], attn_out[0],
    )
    return jnp.stack([one.reshape(1, 1, H, W, C) for one in out])


def solution(mesh):
    return jax.shard_map(
        shards,
        mesh=mesh,
        in_specs=(
            P(None, "seq", None, None, None),
            P(),
            P("section", "seq", None, None, None),
            P("section", None, None, None, None),
            P("section", None, None, None, None),
            P("section", None, None),
            P("section", None, None),
        ),
        out_specs=P(None, "section", "seq", None, None, None),
        check_vma=False,
    )
```

time: 87.9 us -> 77.5 us (0.88)
  Pallas kernels: 85.6 us -> 74.6 us
  other arithmetic: 0 us -> 2.24 us
  local copies, waits for them, and re-layouts: 2.17 us -> 0 us
    pallas_call x1, Pallas kernels: 85.6 us -> 74.6 us  [shards(): pl.pallas_call(body, out_shape=[jax.ShapeDtypeStruct((CELLS, C), BF16)] *...]
    another operation x0 -> x1, other arithmetic: none -> 2.24 us  [shards(): return jnp.stack([one.reshape(1, 1, H, W, C) for one in out])]
    unnamed x1 -> x0, local copies, waits for them, and re-layouts: 2.17 us -> none
where the time goes in v1:
time: 77.5 us; the launch traced here: 76.9 us
  Pallas kernels  74.6 us (96%)
  other arithmetic  2.24 us (3%)
    pallas_call x1, Pallas kernels, shards(): pl.pallas_call(body, out_shape=[jax.ShapeDtypeStruct((CELLS, C), BF16)] *...  74.6 us
    another operation x1, other arithmetic, shards(): return jnp.stack([one.reshape(1, 1, H, W, C) for one in out])  2.24 us

profile of v1, /device:TPU:32, one launch (start us, length us, event | category | flops | bytes accessed | tf_op | source)
XLA Modules:
  0.0 76.9 jit_solution(9863239031030483649)
XLA Ops:
  0.0 74.6 %shard_map.73 = (bf16[384,320]{1,0:T(8,128)(2,1)}, bf16[384,320]{1,0:T(8,128)(2,1)}, bf16[384,320]{1,0:T(8,128)(2,1)}) custom-call(bf16[4,384,320]{2,1,0:T(8,128)(2,1)} %bitcast.11, s32[4]{0:T(128)} %plan.1, bf16[384,320]{1,0:T(8,128)(2,1)} %bitcast.13, bf16[2,9,320,320]{3,2,1,0:T(8,128)(2,1)} %bitcast.9, bf16[2,3,320,320]{3,2,1,0:T(8,128)(2,1)} %bitcast.10, ...), custom_call_target="tpu_custom_call" | custom-call | tf_op jit(solution)/shard_map/pallas_call | solution.py:395
  74.6 2.2 %pad_maximum_fusion = bf16[3,1,1,16,24,320]{5,4,3,2,1,0:T(8,128)(2,1)} fusion(bf16[1,1,1,16,24,320]{5,4,3,2,1,0:T(8,128)(2,1)} %bitcast.16, bf16[1,1,1,16,24,320]{5,4,3,2,1,0:T(8,128)(2,1)} %bitcast.15, bf16[1,1,1,16,24,320]{5,4,3,2,1,0:T(8,128)(2,1)} %bitcast.14), kind=kLoop, calls=%fused_computation | loop fusion | flops 737280 | bytes 1474560 | tf_op jit(solution)/shard_map/stack | solution.py:433

commit v2 on v1

v2 whole, which is shorter than its diff:
```python
import jax
import jax.numpy as jnp
from jax import lax
from jax.experimental import pallas as pl
from jax.experimental.pallas import tpu as pltpu
from jax.sharding import PartitionSpec as P

TICKS = 3
SEQ = 32
NY = 4
NZ = 8
SECTIONS = 8
EPSILON = 1e-05
C = 320
CM = 256
CT = 64
CP = 384
LANES = 128
DEEP = 1024
W = 24
H = 16
CELLS = H * W
NA = 4
NB = 2
ROWS_A = SEQ * NA * 2
ROWS_B = SEQ * NB * 2
BLOCK = 128
PIVOT = ROWS_A
FAR = -1e30
MESH = pl.DeviceIdType.MESH
F32 = jnp.float32
BF16 = jnp.bfloat16


def hops(offset):
    dz, dy = offset
    return min(dz, NZ - dz) + min(dy, NY - dy)


OFFSETS = sorted(
    [(dz, dy) for dz in range(NZ) for dy in range(NY) if (dz, dy) != (0, 0)], key=lambda o: -hops(o)
)


def dot(a, b):
    return jnp.dot(a, b, preferred_element_type=F32)


def in_low(rows):
    return lax.broadcasted_iota(jnp.int32, (rows, LANES), 1) < CT


def turn(v):
    return pltpu.roll(v, CT, 1)


def widen(v):
    return jnp.concatenate([v, jnp.zeros((v.shape[0], CP - C), v.dtype)], axis=1)


def silu_of_half(h):
    return h * jnp.tanh(h) + h


def layer_norm(v, factor):
    center = jnp.sum(v, axis=-1, keepdims=True) * (1.0 / C)
    side = jnp.where(in_low(v.shape[0]), v[:, CM:] - center, 0.0)
    d = jnp.concatenate([v[:, :CM] - center, side], axis=1)
    spread = jnp.sum(d * d, axis=-1, keepdims=True) * (1.0 / C)
    return d * (factor * lax.rsqrt(spread + EPSILON))


def over_groups(rows, groups):
    high = rows.astype(BF16).astype(F32)
    rest = rows - high
    mid = rest.astype(BF16).astype(F32)
    low = rest - mid
    parts = jnp.concatenate([high, mid, low, jnp.zeros_like(low)], axis=0).astype(BF16)
    got = dot(parts, groups)
    return got[0:2] + got[2:4] + got[4:6]


def find_pivot(v, groups):
    total = jnp.sum(v, axis=0, keepdims=True)
    return over_groups(jnp.concatenate([total, total], axis=0), groups)[0:1] * (1.0 / (v.shape[0] * 10))


def group_norm_half(v, pivot, groups):
    count = 1.0 / (CELLS * 10)
    d = v - pivot
    sums = jnp.concatenate([jnp.sum(d, axis=0, keepdims=True), jnp.sum(d * d, axis=0, keepdims=True)], axis=0)
    means = over_groups(sums, groups) * count
    shift = means[0:1]
    spread = jnp.maximum(means[1:2] - shift * shift, 0.0)
    scale = 0.5 * lax.rsqrt(spread + EPSILON)
    return d * scale - shift * scale


def fill_taps(y, x_ref):
    main = y[:, :CM].astype(BF16)
    x_ref[W:, 0:CM] = main[: CELLS - W]
    x_ref[:, CM : 2 * CM] = main
    x_ref[: CELLS - W, 2 * CM : 3 * CM] = main[W:]
    tail = y[:, CM:]
    edge = jnp.zeros((W, LANES), F32)
    above = jnp.concatenate([edge, tail[: CELLS - W]], axis=0)
    below = jnp.concatenate([tail[W:], edge], axis=0)
    x_ref[:, 3 * CM : 3 * CM + LANES] = (above + turn(tail)).astype(BF16)
    x_ref[:, 3 * CM + LANES :] = below.astype(BF16)


def column_taps(p):
    rows = p.shape[0]
    high = rows // W

    def add(left, mid, right):
        width = left.shape[1]
        col = lax.broadcasted_iota(jnp.int32, (high, W, width), 1)
        left = pltpu.roll(left, 1, 0).reshape(high, W, width)
        right = pltpu.roll(right, rows - 1, 0).reshape(high, W, width)
        left = jnp.where(col > 0, left, 0.0).reshape(rows, width)
        right = jnp.where(col < W - 1, right, 0.0).reshape(rows, width)
        return mid + left + right

    main = add(p[:, 0:CM], p[:, CM : 2 * CM], p[:, 2 * CM : 3 * CM])
    pair = p[:, 3 * CM : 3 * CM + LANES]
    tail = jnp.where(in_low(rows), add(pair, turn(pair), p[:, 3 * CM + LANES :]), 0.0)
    return jnp.concatenate([main, tail], axis=1)


def pack(v):
    half = v.shape[0] // 2
    low, high = v[:half], v[half:]
    return jnp.concatenate([low[:, :CM], high[:, :CM], low[:, CM:] + turn(high[:, CM:])], axis=1).astype(BF16)


def unpack(p):
    p = p.astype(F32)
    side = p[:, 2 * CM :]
    mask = in_low(p.shape[0])
    low = jnp.concatenate([p[:, :CM], jnp.where(mask, side, 0.0)], axis=1)
    high = jnp.concatenate([p[:, CM : 2 * CM], jnp.where(mask, turn(side), 0.0)], axis=1)
    return jnp.concatenate([low, high], axis=0)


def temporal_dot(act, cells, w):
    rows = act.shape[0]
    half = rows // 2
    row = lax.broadcasted_iota(jnp.int32, act.shape, 0) & (half - 1)
    before = jnp.where(row >= cells, pltpu.roll(act, cells, 0), 0.0)
    after = jnp.where(row < half - cells, pltpu.roll(act, rows - cells, 0), 0.0)
    lhs = jnp.concatenate(
        [before[:, :CM], act[:, :CM], after[:, :CM], before[:, CM:] + turn(act[:, CM:]), after[:, CM:]], axis=1
    )
    return dot(lhs.astype(BF16), w)


def attention(proj, bias):
    low = in_low(BLOCK)
    scale = 0.125 * 1.4426950408889634
    scores, held = [], []
    for pair in range(3):
        q = proj[:, 128 * pair : 128 * pair + 128]
        k = proj[:, 384 + 128 * pair : 512 + 128 * pair].astype(BF16)
        v = (proj[:, 768 + 128 * pair : 896 + 128 * pair] if pair < 2 else turn(q)).T.astype(BF16)
        for side in range(2 if pair < 2 else 1):
            own = low if side == 0 else jnp.logical_not(low)
            one = jnp.where(own, q, 0.0).astype(BF16)
            scores.append(lax.dot_general(k, one, (((1,), (1,)), ((), ())), preferred_element_type=F32) + bias)
            held.append(v[CT * side : CT * side + CT])
    tops = [jnp.max(s, axis=0, keepdims=True) for s in scores]
    weights = [jnp.exp2((s - top) * scale) for s, top in zip(scores, tops)]
    totals = [jnp.sum(w, axis=0, keepdims=True) for w in weights]
    mixed = [dot(v, w.astype(BF16)) * (1.0 / total) for v, w, total in zip(held, weights, totals)]
    return jnp.concatenate(mixed + [jnp.zeros((CT, BLOCK), F32)], axis=0).T.astype(BF16)


def temporal_part(x1, cells, tw_ref, wi_ref, wo_ref, bias_ref):
    u = temporal_dot(silu_of_half(layer_norm(x1, 0.5)), cells, tw_ref[0]).astype(BF16).astype(F32)
    x2 = (x1 + temporal_dot(silu_of_half(layer_norm(u, 0.5)), cells, tw_ref[1])).astype(BF16).astype(F32)
    proj = dot(layer_norm(x2, 1.0).astype(BF16), wi_ref[...])
    bias = bias_ref[...]
    mixed = [attention(proj[at : at + BLOCK], bias) for at in range(0, x1.shape[0], BLOCK)]
    mixed = mixed[0] if len(mixed) == 1 else jnp.concatenate(mixed, axis=0)
    return x2 + dot(mixed, wo_ref[...])


def body(
    inc_hbm, plan, wait_hbm, sw_hbm, tw_hbm, ai_hbm, ao_hbm, out_ref,
    inc, xi, xs, sw, tws, ai, ao, wc, tw, wi, wo, groups, pivot, bias_a, bias_b, taps,
    sa, sb, fa, fb, ta, tb, ra, rb,
    in_sem, fs_sem, fr_sem, rs_sem, rr_sem, os_sem, or_sem, ready,
):
    me = lax.axis_index("seq")
    section = lax.axis_index("section")
    nxt = lax.rem(section + 1, SECTIONS)
    prv = lax.rem(section + SECTIONS - 1, SECTIONS)
    my_z = me // NY
    my_y = lax.rem(me, NY)

    def peer(offset):
        dz, dy = offset
        return lax.rem(my_z + dz, NZ) * NY + lax.rem(my_y + dy, NY)

    barrier = pltpu.get_barrier_semaphore()
    for offset in OFFSETS:
        pl.semaphore_signal(barrier, 1, device_id={"section": section, "seq": peer(offset)}, device_id_type=MESH)
    for other in (nxt, prv):
        pl.semaphore_signal(barrier, 1, device_id={"section": other, "seq": me}, device_id_type=MESH)

    loads = [
        pltpu.make_async_copy(wait_hbm, xi, in_sem.at[0]),
        pltpu.make_async_copy(sw_hbm.at[0], sw.at[0], in_sem.at[1]),
        pltpu.make_async_copy(sw_hbm.at[1], sw.at[1], in_sem.at[2]),
        pltpu.make_async_copy(ai_hbm, ai, in_sem.at[3]),
        pltpu.make_async_copy(ao_hbm, ao, in_sem.at[4]),
        pltpu.make_async_copy(inc_hbm, inc, in_sem.at[5]),
    ]
    loads.append(pltpu.make_async_copy(tw_hbm, tws, in_sem.at[6]))
    for load in loads:
        load.start()

    row = lax.broadcasted_iota(jnp.int32, (CP, CP), 0)
    col = lax.broadcasted_iota(jnp.int32, (CP, CP), 1)
    groups[...] = jnp.where(((row * 6554) // 65536 == (col * 6554) // 65536) & (row < C), 1.0, 0.0).astype(BF16)
    taps[0:W, 0:CM] = jnp.zeros((W, CM), BF16)
    taps[CELLS - W :, 2 * CM : 3 * CM] = jnp.zeros((W, CM), BF16)

    def make_bias():
        r = lax.broadcasted_iota(jnp.int32, (BLOCK, BLOCK), 0)
        c = lax.broadcasted_iota(jnp.int32, (BLOCK, BLOCK), 1)
        bias_a[...] = jnp.where((r & (NA - 1)) == (c & (NA - 1)), 0.0, FAR)
        half = SEQ * NB
        same = ((r & (NB - 1)) == (c & (NB - 1))) & ((r & half) == (c & half))
        bias_b[...] = jnp.where(same, 0.0, FAR)

    def pack_conv(k):
        for i in range(3):
            part = [widen(sw[k, 3 * i + j]) for j in range(3)]
            side = [t[:, CM:].astype(F32) for t in part]
            whole = jnp.concatenate(
                [t[:, :CM] for t in part] + [(side[0] + turn(side[1])).astype(BF16), part[2][:, CM:]], axis=1)
            wc[k, CM * i : CM * i + CM] = whole[:CM]
            wc[k, 3 * CM + CT * i : 3 * CM + CT * i + CT] = whole[CM:]
        wc[k, 3 * C :] = jnp.zeros((DEEP - 3 * C, DEEP), BF16)

    def pack_temporal():
        for k in range(2):
            for i in range(3):
                part = widen(tws[k, i])
                tw[k, CM * i : CM * i + CM] = part[:CM]
                tw[k, 3 * CM + CT * i : 3 * CM + CT * i + CT] = part[CM:]
            tw[k, 3 * C :] = jnp.zeros((DEEP - 3 * C, CP), BF16)

    def pack_attn():
        whole = ai[...].astype(F32)
        cross = whole[:, 256:384]
        mid = whole[:, 384:640]
        last = jnp.concatenate([whole[:, 896:960], jnp.zeros((C, CT), F32)], axis=1)
        low = in_low(C)
        turned = [turn(t) for t in (cross, mid[:, :128], mid[:, 128:])]
        wi[:C, 0:256] = ai[:, :256]
        wi[:C, 256:384] = jnp.where(low, cross, turn(last)).astype(BF16)
        wi[:C, 384:512] = jnp.where(low, turned[0], turned[1]).astype(BF16)
        wi[:C, 512:640] = jnp.where(low, turned[1], turned[2]).astype(BF16)
        wi[:C, 640:768] = jnp.where(low, turned[2], 0.0).astype(BF16)
        wi[:C, 768:1024] = ai[:, 640:896]
        wi[C:] = jnp.zeros((CP - C, DEEP), BF16)
        wo[:C] = widen(ao[...])
        wo[C:] = jnp.zeros((CP - C, CP), BF16)

    def send_all(t, src, dst, to_section, send_sem, recv_sem):
        for offset in OFFSETS:
            to = peer(offset)
            pltpu.make_async_remote_copy(
                src.at[t, to], dst.at[t, me], send_sem, recv_sem,
                device_id={"section": to_section, "seq": to}, device_id_type=MESH).start()

    def send_forward(t, src, dst, lane):
        send_all(t, src, dst, section, fs_sem.at[lane, t], fr_sem.at[lane, t])
        pltpu.make_async_copy(src.at[t, me], dst.at[t, me], fr_sem.at[lane, t]).start()

    def send_back(t, src, dst, lane):
        target = jnp.where(t < TICKS - 1, nxt, section)
        send_all(t, src, dst, target, rs_sem.at[lane, t], rr_sem.at[lane, t])

        @pl.when(t < TICKS - 1)
        def _():
            pltpu.make_async_remote_copy(
                src.at[t, me], dst.at[t, me], rs_sem.at[lane, t], rr_sem.at[lane, t],
                device_id={"section": target, "seq": me}, device_id_type=MESH).start()

        @pl.when(t == TICKS - 1)
        def _():
            pltpu.make_async_copy(src.at[t, me], dst.at[t, me], rr_sem.at[lane, t]).start()

    def whole(ref, sem):
        pltpu.make_async_copy(ref, ref, sem).wait()

    loads[0].wait()
    pivot[...] = find_pivot(widen(xi[ROWS_A:].astype(F32)), groups[...])

    def tick(t, carry):
        x = widen(xi[...].astype(F32))
        fill_taps(silu_of_half(group_norm_half(x, pivot[...], groups[...])), taps)

        @pl.when(t == 0)
        def _():
            loads[1].wait()
            pack_conv(0)
            loads[2].wait()
            pack_conv(1)

        top = 11 * W
        a = column_taps(dot(taps[...], wc[0])).astype(BF16).astype(F32)
        fill_taps(silu_of_half(group_norm_half(a, find_pivot(a[:PIVOT], groups[...]), groups[...])), taps)
        got = column_taps(dot(taps[top - W :], wc[1]))
        sb[t] = pack(x[ROWS_A:] + got[ROWS_A - top + W :]).reshape(SEQ, NB, 2 * C)

        @pl.when(t == 0)
        def _():
            pl.semaphore_wait(barrier, SEQ + 1)

        send_forward(t, sb, fb, 1)
        got = column_taps(dot(taps[0:top], wc[1]))
        sa[t] = pack(x[:ROWS_A] + got[:ROWS_A]).reshape(SEQ, NA, 2 * C)
        send_forward(t, sa, fa, 0)

        @pl.when(t == 0)
        def _():
            make_bias()
            for load in loads[3:]:
                load.wait()
            pack_temporal()
            pack_attn()

        whole(fb.at[t], fr_sem.at[1, t])

        @pl.when(t == 0)
        def _():
            pl.semaphore_signal(ready, 1, device_id={"section": prv, "seq": me}, device_id_type=MESH)

        done = temporal_part(unpack(fb[t].reshape(SEQ * NB, 2 * C)), NB, tw, wi, wo, bias_b)
        tb[t] = pack(done).reshape(SEQ, NB, 2 * C)

        @pl.when(t == 0)
        def _():
            pl.semaphore_wait(ready, 1)

        send_back(t, tb, rb, 1)
        whole(fa.at[t], fr_sem.at[0, t])
        done = temporal_part(unpack(fa[t].reshape(SEQ * NA, 2 * C)), NA, tw, wi, wo, bias_a)
        ta[t] = pack(done).reshape(SEQ, NA, 2 * C)
        send_back(t, ta, ra, 0)
        whole(rb.at[t], rr_sem.at[1, t])
        came = unpack(rb[t].reshape(SEQ * NB, 2 * C))[:, :C].astype(BF16)
        xs[t, ROWS_A:] = came
        came = jnp.where(section == 0, inc[plan[t], ROWS_A:], came)
        xi[ROWS_A:] = came
        pivot[...] = find_pivot(widen(came.astype(F32)), groups[...])
        whole(ra.at[t], rr_sem.at[0, t])
        came = unpack(ra[t].reshape(SEQ * NA, 2 * C))[:, :C].astype(BF16)
        xs[t, 0:ROWS_A] = came

        @pl.when(t < TICKS - 1)
        def _():
            pltpu.make_async_remote_copy(
                xs.at[t], out_ref.at[t], os_sem.at[t], or_sem.at[t],
                device_id={"section": prv, "seq": me}, device_id_type=MESH).start()
            xi[0:ROWS_A] = jnp.where(section == 0, inc[plan[t], 0:ROWS_A], xs[t, 0:ROWS_A])

        return carry

    lax.fori_loop(0, TICKS, tick, 0)
    out_ref[TICKS - 1] = xs[TICKS - 1]
    for t in range(TICKS):
        for lane, (src, back) in enumerate(((sa, ta), (sb, tb))):
            part = src.at[t, pl.ds(0, SEQ - 1)]
            pltpu.make_async_copy(part, part, fs_sem.at[lane, t]).wait()
            part = back.at[t, pl.ds(0, SEQ - 1 if t == TICKS - 1 else SEQ)]
            pltpu.make_async_copy(part, part, rs_sem.at[lane, t]).wait()
    for t in range(TICKS - 1):
        pltpu.make_async_copy(xs.at[t], xs.at[t], os_sem.at[t]).wait()
        pltpu.make_async_copy(out_ref.at[t], out_ref.at[t], or_sem.at[t]).wait()


def shards(incoming, plan, waiting, spatial_weight, temporal_weight, attn_in, attn_out):
    hbm = pl.BlockSpec(memory_space=pl.ANY)
    steps = (TICKS,)
    out = pl.pallas_call(
        body,
        out_shape=pltpu.VMEM((TICKS, CELLS, C), BF16),
        in_specs=[hbm, pl.BlockSpec(memory_space=pltpu.SMEM), hbm, hbm, hbm, hbm, hbm],
        out_specs=pl.BlockSpec(memory_space=pltpu.VMEM),
        scratch_shapes=[
            pltpu.VMEM((4, CELLS, C), BF16),
            pltpu.VMEM((CELLS, C), BF16),
            pltpu.VMEM(steps + (CELLS, C), BF16),
            pltpu.VMEM((2, 9, C, C), BF16),
            pltpu.VMEM((2, 3, C, C), BF16),
            pltpu.VMEM((C, 3 * C), BF16),
            pltpu.VMEM((C, C), BF16),
            pltpu.VMEM((2, DEEP, DEEP), BF16),
            pltpu.VMEM((2, DEEP, CP), BF16),
            pltpu.VMEM((CP, DEEP), BF16),
            pltpu.VMEM((CP, CP), BF16),
            pltpu.VMEM((CP, CP), BF16),
            pltpu.VMEM((1, CP), F32),
            pltpu.VMEM((BLOCK, BLOCK), F32),
            pltpu.VMEM((BLOCK, BLOCK), F32),
            pltpu.VMEM((CELLS, DEEP), BF16),
        ]
        + [pltpu.VMEM(steps + (SEQ, n, 2 * C), BF16) for _ in range(4) for n in (NA, NB)]
        + [
            pltpu.SemaphoreType.DMA((7,)),
            pltpu.SemaphoreType.DMA((2, TICKS)),
            pltpu.SemaphoreType.DMA((2, TICKS)),
            pltpu.SemaphoreType.DMA((2, TICKS)),
            pltpu.SemaphoreType.DMA((2, TICKS)),
            pltpu.SemaphoreType.DMA((TICKS - 1,)),
            pltpu.SemaphoreType.DMA((TICKS - 1,)),
            pltpu.SemaphoreType.REGULAR,
        ],
        compiler_params=pltpu.CompilerParams(
            collective_id=0, has_side_effects=True, vmem_limit_bytes=60 * 1024 * 1024),
    )(
        incoming.reshape(4, CELLS, C), plan, waiting.reshape(CELLS, C),
        spatial_weight[0], temporal_weight[0], attn_in[0], attn_out[0],
    )
    return out.reshape(TICKS, 1, 1, H, W, C)


def solution(mesh):
    return jax.shard_map(
        shards,
        mesh=mesh,
        in_specs=(
            P(None, "seq", None, None, None),
            P(),
            P("section", "seq", None, None, None),
            P("section", None, None, None, None),
            P("section", None, None, None, None),
            P("section", None, None),
            P("section", None, None),
        ),
        out_specs=P(None, "section", "seq", None, None, None),
        check_vma=False,
    )
```

time: 77.5 us -> 71.3 us (0.920)
  Pallas kernels: 74.6 us -> 70.3 us
  other arithmetic: 2.24 us -> 0 us
  local copies, waits for them, and re-layouts: 0 us -> 0.91 us
    pallas_call x1, Pallas kernels: 74.6 us -> 70.3 us  [shards(): pl.pallas_call(body, out_shape=pltpu.VMEM((TICKS, CELLS, C), BF16), in_sp...]
    another operation x1 -> x0, other arithmetic: 2.24 us -> none  [shards(): return jnp.stack([one.reshape(1, 1, H, W, C) for one in out])]
    unnamed x0 -> x1, local copies, waits for them, and re-layouts: none -> 0.91 us
where the time goes in v2:
time: 71.3 us; the launch traced here: 71.2 us
  Pallas kernels  70.3 us (99%)
  local copies, waits for them, and re-layouts  0.91 us (1%)
    pallas_call x1, Pallas kernels, shards(): pl.pallas_call(body, out_shape=pltpu.VMEM((TICKS, CELLS, C), BF16), in_sp...  70.3 us

profile of v2, /device:TPU:32, one launch (start us, length us, event | category | flops | bytes accessed | tf_op | source)
XLA Modules:
  0.0 71.2 jit_solution(997034339291315496)
XLA Ops:
  0.0 70.3 %shard_map.73 = bf16[3,384,320]{2,1,0:T(8,128)(2,1)S(1)} custom-call(bf16[4,384,320]{2,1,0:T(8,128)(2,1)} %bitcast.12, s32[4]{0:T(128)} %plan.1, bf16[384,320]{1,0:T(8,128)(2,1)} %bitcast.14, bf16[2,9,320,320]{3,2,1,0:T(8,128)(2,1)} %bitcast.10, bf16[2,3,320,320]{3,2,1,0:T(8,128)(2,1)} %bitcast.11, bf16[320,960]{1,0:T(8,128)(2,1)} %bitcast.13, ...), custom_call_target="tpu_custom_call" | custom-call | tf_op jit(solution)/shard_map/pallas_call | solution.py:390
  70.3 0.9 %copy.10 = bf16[3,1,1,16,24,320]{5,4,3,2,1,0:T(8,128)(2,1)} copy(bf16[3,1,1,16,24,320]{5,4,3,2,1,0:T(8,128)(2,1)S(1)} %bitcast.9) | data formatting | bytes 1474560

commit v3 on v2

--- a/solution.py
+++ b/solution.py
@@ -143,16 +143,14 @@
     return jnp.concatenate([low, high], axis=0)
 
 
-def temporal_dot(act, cells, w):
+def temporal_taps(act, cells, half):
     rows = act.shape[0]
-    half = rows // 2
     row = lax.broadcasted_iota(jnp.int32, act.shape, 0) & (half - 1)
     before = jnp.where(row >= cells, pltpu.roll(act, cells, 0), 0.0)
     after = jnp.where(row < half - cells, pltpu.roll(act, rows - cells, 0), 0.0)
-    lhs = jnp.concatenate(
+    return jnp.concatenate(
         [before[:, :CM], act[:, :CM], after[:, :CM], before[:, CM:] + turn(act[:, CM:]), after[:, CM:]], axis=1
-    )
-    return dot(lhs.astype(BF16), w)
+    ).astype(BF16)
 
 
 def attention(proj, bias):
@@ -176,18 +174,23 @@
 
 
 def temporal_part(x1, cells, tw_ref, wi_ref, wo_ref, bias_ref):
-    u = temporal_dot(silu_of_half(layer_norm(x1, 0.5)), cells, tw_ref[0]).astype(BF16).astype(F32)
-    x2 = (x1 + temporal_dot(silu_of_half(layer_norm(u, 0.5)), cells, tw_ref[1])).astype(BF16).astype(F32)
-    proj = dot(layer_norm(x2, 1.0).astype(BF16), wi_ref[...])
+    half = x1.shape[0] // 2
     bias = bias_ref[...]
-    mixed = [attention(proj[at : at + BLOCK], bias) for at in range(0, x1.shape[0], BLOCK)]
-    mixed = mixed[0] if len(mixed) == 1 else jnp.concatenate(mixed, axis=0)
-    return x2 + dot(mixed, wo_ref[...])
+    x1 = [x1[at : at + BLOCK] for at in range(0, 2 * half, BLOCK)]
+    taps = [temporal_taps(silu_of_half(layer_norm(v, 0.5)), cells, half) for v in x1]
+    u = [dot(v, tw_ref[0]).astype(BF16).astype(F32) for v in taps]
+    taps = [temporal_taps(silu_of_half(layer_norm(v, 0.5)), cells, half) for v in u]
+    x2 = [(v + dot(tap, tw_ref[1])).astype(BF16).astype(F32) for v, tap in zip(x1, taps)]
+    normed = [layer_norm(v, 1.0).astype(BF16) for v in x2]
+    proj = [dot(v, wi_ref[...]) for v in normed]
+    mixed = [attention(v, bias) for v in proj]
+    done = [v + dot(mix, wo_ref[...]) for v, mix in zip(x2, mixed)]
+    return done[0] if len(done) == 1 else jnp.concatenate(done, axis=0)
 
 
 def body(
-    inc_hbm, plan, wait_hbm, sw_hbm, tw_hbm, ai_hbm, ao_hbm, out_ref,
-    inc, xi, xs, sw, tws, ai, ao, wc, tw, wi, wo, groups, pivot, bias_a, bias_b, taps,
+    inc_hbm, plan_hbm, wait_hbm, sw_hbm, tw_hbm, ai_hbm, ao_hbm, out_ref,
+    plan, inc, xi, xs, sw, tws, ai, ao, wc, tw, wi, wo, groups, pivot, bias_a, bias_b, taps,
     sa, sb, fa, fb, ta, tb, ra, rb,
     in_sem, fs_sem, fr_sem, rs_sem, rr_sem, os_sem, or_sem, ready,
 ):
@@ -202,12 +205,6 @@
         dz, dy = offset
         return lax.rem(my_z + dz, NZ) * NY + lax.rem(my_y + dy, NY)
 
-    barrier = pltpu.get_barrier_semaphore()
-    for offset in OFFSETS:
-        pl.semaphore_signal(barrier, 1, device_id={"section": section, "seq": peer(offset)}, device_id_type=MESH)
-    for other in (nxt, prv):
-        pl.semaphore_signal(barrier, 1, device_id={"section": other, "seq": me}, device_id_type=MESH)
-
     loads = [
         pltpu.make_async_copy(wait_hbm, xi, in_sem.at[0]),
         pltpu.make_async_copy(sw_hbm.at[0], sw.at[0], in_sem.at[1]),
@@ -217,7 +214,17 @@
         pltpu.make_async_copy(inc_hbm, inc, in_sem.at[5]),
     ]
     loads.append(pltpu.make_async_copy(tw_hbm, tws, in_sem.at[6]))
-    for load in loads:
+    loads.append(pltpu.make_async_copy(plan_hbm, plan, in_sem.at[7]))
+    for load in loads[:3]:
+        load.start()
+
+    barrier = pltpu.get_barrier_semaphore()
+    for offset in OFFSETS:
+        pl.semaphore_signal(barrier, 1, device_id={"section": section, "seq": peer(offset)}, device_id_type=MESH)
+    for other in (nxt, prv):
+        pl.semaphore_signal(barrier, 1, device_id={"section": other, "seq": me}, device_id_type=MESH)
+
+    for load in loads[3:]:
         load.start()
 
     row = lax.broadcasted_iota(jnp.int32, (CP, CP), 0)
@@ -281,53 +288,42 @@
         pltpu.make_async_copy(src.at[t, me], dst.at[t, me], fr_sem.at[lane, t]).start()
 
     def send_back(t, src, dst, lane):
-        target = jnp.where(t < TICKS - 1, nxt, section)
-        send_all(t, src, dst, target, rs_sem.at[lane, t], rr_sem.at[lane, t])
-
-        @pl.when(t < TICKS - 1)
-        def _():
+        if t == TICKS - 1:
+            send_all(t, src, dst, section, rs_sem.at[lane, t], rr_sem.at[lane, t])
+            pltpu.make_async_copy(src.at[t, me], dst.at[t, me], rr_sem.at[lane, t]).start()
+        else:
+            send_all(t, src, dst, nxt, rs_sem.at[lane, t], rr_sem.at[lane, t])
             pltpu.make_async_remote_copy(
                 src.at[t, me], dst.at[t, me], rs_sem.at[lane, t], rr_sem.at[lane, t],
-                device_id={"section": target, "seq": me}, device_id_type=MESH).start()
-
-        @pl.when(t == TICKS - 1)
-        def _():
-            pltpu.make_async_copy(src.at[t, me], dst.at[t, me], rr_sem.at[lane, t]).start()
+                device_id={"section": nxt, "seq": me}, device_id_type=MESH).start()
 
     def whole(ref, sem):
         pltpu.make_async_copy(ref, ref, sem).wait()
 
     loads[0].wait()
     pivot[...] = find_pivot(widen(xi[ROWS_A:].astype(F32)), groups[...])
-
-    def tick(t, carry):
+    top = 11 * W
+    for t in range(TICKS):
         x = widen(xi[...].astype(F32))
         fill_taps(silu_of_half(group_norm_half(x, pivot[...], groups[...])), taps)
-
-        @pl.when(t == 0)
-        def _():
+        if t == 0:
             loads[1].wait()
             pack_conv(0)
+        p = dot(taps[...], wc[0])
+        if t == 0:
             loads[2].wait()
             pack_conv(1)
-
-        top = 11 * W
-        a = column_taps(dot(taps[...], wc[0])).astype(BF16).astype(F32)
+        a = column_taps(p).astype(BF16).astype(F32)
         fill_taps(silu_of_half(group_norm_half(a, find_pivot(a[:PIVOT], groups[...]), groups[...])), taps)
         got = column_taps(dot(taps[top - W :], wc[1]))
         sb[t] = pack(x[ROWS_A:] + got[ROWS_A - top + W :]).reshape(SEQ, NB, 2 * C)
-
-        @pl.when(t == 0)
-        def _():
+        if t == 0:
             pl.semaphore_wait(barrier, SEQ + 1)
-
         send_forward(t, sb, fb, 1)
         got = column_taps(dot(taps[0:top], wc[1]))
         sa[t] = pack(x[:ROWS_A] + got[:ROWS_A]).reshape(SEQ, NA, 2 * C)
         send_forward(t, sa, fa, 0)
-
-        @pl.when(t == 0)
-        def _():
+        if t == 0:
             make_bias()
             for load in loads[3:]:
                 load.wait()
@@ -335,44 +331,37 @@
             pack_attn()
 
         whole(fb.at[t], fr_sem.at[1, t])
-
-        @pl.when(t == 0)
-        def _():
+        if t == 0:
             pl.semaphore_signal(ready, 1, device_id={"section": prv, "seq": me}, device_id_type=MESH)
-
         done = temporal_part(unpack(fb[t].reshape(SEQ * NB, 2 * C)), NB, tw, wi, wo, bias_b)
         tb[t] = pack(done).reshape(SEQ, NB, 2 * C)
-
-        @pl.when(t == 0)
-        def _():
+        if t == 0:
             pl.semaphore_wait(ready, 1)
-
         send_back(t, tb, rb, 1)
         whole(fa.at[t], fr_sem.at[0, t])
         done = temporal_part(unpack(fa[t].reshape(SEQ * NA, 2 * C)), NA, tw, wi, wo, bias_a)
         ta[t] = pack(done).reshape(SEQ, NA, 2 * C)
         send_back(t, ta, ra, 0)
+
         whole(rb.at[t], rr_sem.at[1, t])
-        came = unpack(rb[t].reshape(SEQ * NB, 2 * C))[:, :C].astype(BF16)
-        xs[t, ROWS_A:] = came
-        came = jnp.where(section == 0, inc[plan[t], ROWS_A:], came)
-        xi[ROWS_A:] = came
-        pivot[...] = find_pivot(widen(came.astype(F32)), groups[...])
+        came_b = unpack(rb[t].reshape(SEQ * NB, 2 * C))[:, :C].astype(BF16)
+        if t == TICKS - 1:
+            out_ref[t, ROWS_A:] = came_b
+            whole(ra.at[t], rr_sem.at[0, t])
+            out_ref[t, 0:ROWS_A] = unpack(ra[t].reshape(SEQ * NA, 2 * C))[:, :C].astype(BF16)
+            break
+        xs[t, ROWS_A:] = came_b
+        came_b = jnp.where(section == 0, inc[plan[t], ROWS_A:], came_b)
+        xi[ROWS_A:] = came_b
+        pivot[...] = find_pivot(widen(came_b.astype(F32)), groups[...])
         whole(ra.at[t], rr_sem.at[0, t])
-        came = unpack(ra[t].reshape(SEQ * NA, 2 * C))[:, :C].astype(BF16)
-        xs[t, 0:ROWS_A] = came
-
-        @pl.when(t < TICKS - 1)
-        def _():
-            pltpu.make_async_remote_copy(
-                xs.at[t], out_ref.at[t], os_sem.at[t], or_sem.at[t],
-                device_id={"section": prv, "seq": me}, device_id_type=MESH).start()
-            xi[0:ROWS_A] = jnp.where(section == 0, inc[plan[t], 0:ROWS_A], xs[t, 0:ROWS_A])
-
-        return carry
-
-    lax.fori_loop(0, TICKS, tick, 0)
-    out_ref[TICKS - 1] = xs[TICKS - 1]
+        came_a = unpack(ra[t].reshape(SEQ * NA, 2 * C))[:, :C].astype(BF16)
+        xs[t, 0:ROWS_A] = came_a
+        xi[0:ROWS_A] = jnp.where(section == 0, inc[plan[t], 0:ROWS_A], came_a)
+        pltpu.make_async_remote_copy(
+            xs.at[t], out_ref.at[t], os_sem.at[t], or_sem.at[t],
+            device_id={"section": prv, "seq": me}, device_id_type=MESH).start()
+
     for t in range(TICKS):
         for lane, (src, back) in enumerate(((sa, ta), (sb, tb))):
             part = src.at[t, pl.ds(0, SEQ - 1)]
@@ -390,12 +379,13 @@
     out = pl.pallas_call(
         body,
         out_shape=pltpu.VMEM((TICKS, CELLS, C), BF16),
-        in_specs=[hbm, pl.BlockSpec(memory_space=pltpu.SMEM), hbm, hbm, hbm, hbm, hbm],
+        in_specs=[hbm] * 7,
         out_specs=pl.BlockSpec(memory_space=pltpu.VMEM),
         scratch_shapes=[
+            pltpu.SMEM((4,), jnp.int32),
             pltpu.VMEM((4, CELLS, C), BF16),
             pltpu.VMEM((CELLS, C), BF16),
-            pltpu.VMEM(steps + (CELLS, C), BF16),
+            pltpu.VMEM((TICKS - 1, CELLS, C), BF16),
             pltpu.VMEM((2, 9, C, C), BF16),
             pltpu.VMEM((2, 3, C, C), BF16),
             pltpu.VMEM((C, 3 * C), BF16),
@@ -412,7 +402,7 @@
         ]
         + [pltpu.VMEM(steps + (SEQ, n, 2 * C), BF16) for _ in range(4) for n in (NA, NB)]
         + [
-            pltpu.SemaphoreType.DMA((7,)),
+            pltpu.SemaphoreType.DMA((8,)),
             pltpu.SemaphoreType.DMA((2, TICKS)),
             pltpu.SemaphoreType.DMA((2, TICKS)),
             pltpu.SemaphoreType.DMA((2, TICKS)),

time: 71.3 us -> 69.1 us (0.969)
  Pallas kernels: 70.3 us -> 67.8 us
    pallas_call x1, Pallas kernels: 70.3 us -> 67.8 us  [shards(): pl.pallas_call(body, out_shape=pltpu.VMEM((TICKS, CELLS, C), BF16), in_sp...]
where the time goes in v3:
time: 69.1 us; the launch traced here: 68.7 us
  Pallas kernels  67.8 us (98%)
  local copies, waits for them, and re-layouts  0.91 us (1%)
    pallas_call x1, Pallas kernels, shards(): pl.pallas_call(body, out_shape=pltpu.VMEM((TICKS, CELLS, C), BF16), in_sp...  67.8 us

profile of v3, /device:TPU:32, one launch (start us, length us, event | category | flops | bytes accessed | tf_op | source)
XLA Modules:
  0.0 68.7 jit_solution(17379804639479741502)
XLA Ops:
  0.0 67.8 %shard_map.73 = bf16[3,384,320]{2,1,0:T(8,128)(2,1)S(1)} custom-call(bf16[4,384,320]{2,1,0:T(8,128)(2,1)} %bitcast.12, s32[4]{0:T(128)} %plan_hbm.1, bf16[384,320]{1,0:T(8,128)(2,1)} %bitcast.14, bf16[2,9,320,320]{3,2,1,0:T(8,128)(2,1)} %bitcast.10, bf16[2,3,320,320]{3,2,1,0:T(8,128)(2,1)} %bitcast.11, bf16[320,960]{1,0:T(8,128)(2,1)} %bitcast.13, ...), custom_call_target="tpu_custom_call" | custom-call | tf_op jit(solution)/shard_map/pallas_call | solution.py:379
  67.8 0.9 %copy.10 = bf16[3,1,1,16,24,320]{5,4,3,2,1,0:T(8,128)(2,1)} copy(bf16[3,1,1,16,24,320]{5,4,3,2,1,0:T(8,128)(2,1)S(1)} %bitcast.9) | data formatting | bytes 1474560

commit v4 on v3

--- a/solution.py
+++ b/solution.py
@@ -309,9 +309,9 @@
         if t == 0:
             loads[1].wait()
             pack_conv(0)
+            loads[2].wait()
         p = dot(taps[...], wc[0])
         if t == 0:
-            loads[2].wait()
             pack_conv(1)
         a = column_taps(p).astype(BF16).astype(F32)
         fill_taps(silu_of_half(group_norm_half(a, find_pivot(a[:PIVOT], groups[...]), groups[...])), taps)

time: 69.1 us -> 69.1 us (level)
  no operation moved by 1% of the time
where the time goes in v4:
time: 69.1 us; the launch traced here: 69 us
  Pallas kernels  68.1 us (99%)
  local copies, waits for them, and re-layouts  0.91 us (1%)
    pallas_call x1, Pallas kernels, shards(): pl.pallas_call(body, out_shape=pltpu.VMEM((TICKS, CELLS, C), BF16), in_sp...  68.1 us

profile of v4, /device:TPU:32, one launch (start us, length us, event | category | flops | bytes accessed | tf_op | source)
XLA Modules:
  0.0 69.0 jit_solution(4098033826590219383)
XLA Ops:
  0.0 68.1 %shard_map.73 = bf16[3,384,320]{2,1,0:T(8,128)(2,1)S(1)} custom-call(bf16[4,384,320]{2,1,0:T(8,128)(2,1)} %bitcast.12, s32[4]{0:T(128)} %plan_hbm.1, bf16[384,320]{1,0:T(8,128)(2,1)} %bitcast.14, bf16[2,9,320,320]{3,2,1,0:T(8,128)(2,1)} %bitcast.10, bf16[2,3,320,320]{3,2,1,0:T(8,128)(2,1)} %bitcast.11, bf16[320,960]{1,0:T(8,128)(2,1)} %bitcast.13, ...), custom_call_target="tpu_custom_call" | custom-call | tf_op jit(solution)/shard_map/pallas_call | solution.py:379
  68.1 0.9 %copy.10 = bf16[3,1,1,16,24,320]{5,4,3,2,1,0:T(8,128)(2,1)} copy(bf16[3,1,1,16,24,320]{5,4,3,2,1,0:T(8,128)(2,1)S(1)} %bitcast.9) | data formatting | bytes 1474560
